TPU v7x, 128 devices: a whole 4x4x4 slice. The times are simulated.
128 devices in a mesh: ctx: 16 (over y, z_hi, core), dp: 8 (over x, z_lo).
Axes of the slice: x: 4, y: 4, z: 4 (z_hi: 2, z_lo: 2; z = z_hi * 2 + z_lo), core: 2. Of those that a mesh axis runs over, the one named last changes fastest.
Arguments:
- tokens: bfloat16 [8, 4096, 16384], P('dp', 'ctx'), may hold values from -6 to 6
- queries: bfloat16 [8, 4096, 1024], P('dp', 'ctx'), may hold values from -200 to 200
- cotangent: bfloat16 [8, 4096, 1024], P('dp', 'ctx'), may hold values from -6 to 6
- latent_key: float32 [16384, 128], P(('ctx', 'dp')), may hold values from -1 to 1
- latent_value: float32 [16384, 128], P(('ctx', 'dp')), may hold values from -1 to 1
- lengths: int32 [8, 8], P('dp'), may hold values from 1 to 2048, 4096 in all within a row
- block_order: int32 [8, 32], P('dp'), may hold values from 0 to 31, each once within a row
Outputs:
- attn_out: bfloat16 [8, 4096, 1024], P('dp', 'ctx')
- query_grad: bfloat16 [8, 4096, 1024], P('dp', 'ctx')
- token_grad: bfloat16 [8, 4096, 16384], P('dp', 'ctx')
- key_weight_grad: float32 [16384, 128], P(('ctx', 'dp'))
- value_weight_grad: float32 [16384, 128], P(('ctx', 'dp'))
Inputs may be any that keep to these rules, and one draw needn't show every extreme that they name: Each row holds the lengths of the 8 documents packed into one sequence, in order; they sum to 4096 and the largest is exactly 2048. Each row is a permutation; stored block b of a sequence (rows b * 128 to (b + 1) * 128 - 1) holds the tokens at positions block_order[b] * 128 to block_order[b] * 128 + 127.
All inputs are finite; a program needn't handle non-finite values. Where the computation divides by a largest or mean magnitude, that divisor is 1e-20 or more.
Results may differ from a plain program's by a relative error of at most 0.02.
The roundings to bfloat16 on the way count: a program that leaves them out, or rounds other values in their place, can miss the bound.
Values may be sent and summed in bfloat16 or wider, within the bound.
No kernel may reach another device: no remote copies, remote signals or barrier semaphores. Data moves between devices by JAX's collectives and lax.ppermute only.
A program may use at most 128 MiB of HBM per device.

v0:
```python
import jax
import jax.numpy as jnp
from jax import lax
from jax.sharding import Mesh
from jax.sharding import PartitionSpec as P

CTX = ("ctx_0", "ctx_1", "ctx_2")
CTX_DP = ("ctx_0", "ctx_1", "ctx_2", "dp_0", "dp_1")
DP = ("dp_0", "dp_1")
EPSILON = 1e-05
NEGATIVE = -1e30


def over_axes(value, axes):
    for axis in axes:
        value = lax.psum(value, axis)
    return value


def in_one_piece(arrays, axis, dim, along):
    both = jnp.concatenate(arrays, axis=along)
    result, at, done = (lax.all_gather(both, axis, axis=dim, tiled=True), 0, [])
    for a in arrays:
        done.append(lax.slice_in_dim(result, at, at + a.shape[along], axis=along))
        at += a.shape[along]
    return tuple(done)


def levels(ratio):
    return jnp.where(ratio >= 0.5, 1.0, jnp.where(ratio <= -0.5, -1.0, 0.0)).astype(jnp.float32)


def over_blocks(advance, state_now, key_rows, value_rows):
    row_total = key_rows.shape[0]
    width_rows = 512
    block_count = row_total // width_rows
    key_blocks = key_rows.reshape(block_count, width_rows, key_rows.shape[1])
    value_blocks = value_rows.reshape(block_count, width_rows, value_rows.shape[1])

    def turn_once(carried, block_item):
        key_block, value_block, number = block_item
        return (advance(carried, key_block, value_block, number * width_rows), None)

    state_now, _ = lax.scan(
        turn_once, state_now, (key_blocks, value_blocks, jnp.arange(block_count, dtype=jnp.int32))
    )
    return state_now


def body(tokens, queries, cotangent, latent_key, latent_value, lengths, block_order):
    token_rows = tokens[0]
    rows_here = token_rows.shape[0]
    head_size = latent_key.shape[1]
    head_count = queries.shape[2] // head_size
    scale_factor = head_size ** (-0.5)
    block_rows = rows_here // 2
    lengths_row = lengths[0]
    order_row = block_order[0]
    block_ids = jnp.arange(order_row.shape[0], dtype=jnp.int32)
    doc_starts = jnp.cumsum(lengths_row, dtype=jnp.int32) - lengths_row

    def positions(stored):
        owner = jnp.sum(
            jnp.where((stored // block_rows)[:, None] == block_ids[None, :], order_row[None, :], 0),
            axis=1,
        )
        return owner * block_rows + stored % block_rows

    def documents(position):
        return jnp.sum((position[:, None] >= doc_starts[None, :]).astype(jnp.int32), axis=1)

    query_pos = positions(lax.axis_index(CTX) * rows_here + jnp.arange(rows_here, dtype=jnp.int32))
    query_doc = documents(query_pos)

    def visibility(first_row, row_total):
        key_pos = positions(first_row + jnp.arange(row_total, dtype=jnp.int32))
        key_doc = documents(key_pos)
        return (key_pos[None, :] <= query_pos[:, None]) & (key_doc[None, :] == query_doc[:, None])

    entry_count = latent_key.shape[0] * lax.axis_size(CTX_DP) * head_size
    magnitudes = (
        over_axes(jnp.sum(jnp.abs(latent_key)), CTX_DP),
        over_axes(jnp.sum(jnp.abs(latent_value)), CTX_DP),
    )
    key_scale = magnitudes[0] / entry_count + EPSILON
    value_scale = magnitudes[1] / entry_count + EPSILON
    local_rows = jnp.concatenate(
        [
            (key_scale * levels(latent_key / key_scale)).astype(jnp.bfloat16),
            (value_scale * levels(latent_value / value_scale)).astype(jnp.bfloat16),
        ],
        axis=1,
    )
    both = lax.all_gather(local_rows, CTX_DP, axis=0, tiled=True)
    projected = jnp.dot(token_rows, both, preferred_element_type=jnp.float32).astype(jnp.bfloat16)
    key_pair = (projected[:, :head_size][None], projected[:, head_size:][None])
    query_heads = queries[0].reshape(rows_here, head_count, head_size)
    cot_heads = cotangent[0].reshape(rows_here, head_count, head_size)

    def forward_block(state_now, key_block, value_block, first_row):
        best, total, accum = state_now
        scores = (
            jnp.einsum("thd,sd->hts", query_heads, key_block, preferred_element_type=jnp.float32)
            * scale_factor
        )
        visible = visibility(first_row, key_block.shape[0])
        scores = jnp.where(visible[None], scores, NEGATIVE)
        new_best = jnp.maximum(best, jnp.max(scores, axis=2))
        weights = jnp.where(visible[None], jnp.exp(scores - new_best[:, :, None]), 0.0)
        shrink = jnp.exp(best - new_best)
        total = total * shrink + jnp.sum(weights, axis=2)
        accum = accum * shrink.T[:, :, None] + jnp.einsum(
            "hts,sd->thd",
            weights.astype(jnp.bfloat16),
            value_block,
            preferred_element_type=jnp.float32,
        )
        return (new_best, total, accum)

    start_state = (
        jnp.full((head_count, rows_here), NEGATIVE, jnp.float32),
        jnp.zeros((head_count, rows_here), jnp.float32),
        jnp.zeros((rows_here, head_count, head_size), jnp.float32),
    )
    shard_part = in_one_piece((key_pair[0], key_pair[1]), CTX, 1, 0)
    state_final = over_blocks(forward_block, start_state, shard_part[0][0], shard_part[1][0])
    all_keys, all_values = in_one_piece((key_pair[0], key_pair[1]), CTX, 1, 0)
    best, total, accum = state_final
    log_total = best + jnp.log(total)
    mixed = (accum / total.T[:, :, None]).astype(jnp.bfloat16)
    expected = jnp.sum(cot_heads.astype(jnp.float32) * mixed.astype(jnp.float32), axis=2).T

    def backward_block(query_acc, key_block, value_block, first_row):
        scores = (
            jnp.einsum("thd,sd->hts", query_heads, key_block, preferred_element_type=jnp.float32)
            * scale_factor
        )
        visible = visibility(first_row, key_block.shape[0])
        probability = jnp.where(visible[None], jnp.exp(scores - log_total[:, :, None]), 0.0)
        prob_grad = jnp.einsum(
            "thd,sd->hts", cot_heads, value_block, preferred_element_type=jnp.float32
        )
        score_grad = (probability * (prob_grad - expected[:, :, None])).astype(jnp.bfloat16)
        query_acc = (
            query_acc
            + jnp.einsum("hts,sd->thd", score_grad, key_block, preferred_element_type=jnp.float32)
            * scale_factor
        )
        key_part = (
            jnp.einsum("hts,thd->sd", score_grad, query_heads, preferred_element_type=jnp.float32)
            * scale_factor
        )
        value_part = jnp.einsum(
            "hts,thd->sd",
            probability.astype(jnp.bfloat16),
            cot_heads,
            preferred_element_type=jnp.float32,
        )
        return (query_acc, jnp.concatenate([key_part, value_part], axis=1))

    key_all = all_keys[0]
    value_all = all_values[0]
    total_rows = key_all.shape[0]
    width_rows = 512
    block_count = total_rows // width_rows

    def backward_turn(query_acc, block_item):
        key_block, value_block, number = block_item
        return backward_block(query_acc, key_block, value_block, number * width_rows)

    query_acc, key_terms = lax.scan(
        backward_turn,
        jnp.zeros((rows_here, head_count, head_size), jnp.float32),
        (
            key_all.reshape(block_count, width_rows, head_size),
            value_all.reshape(block_count, width_rows, head_size),
            jnp.arange(block_count, dtype=jnp.int32),
        ),
    )
    key_terms = key_terms.reshape(total_rows, 2 * head_size)
    grads_kv = lax.psum_scatter(key_terms, CTX, scatter_dimension=0, tiled=True).astype(
        jnp.bfloat16
    )
    token_grad = lax.dot_general(
        grads_kv, both, (((1,), (1,)), ((), ())), preferred_element_type=jnp.float32
    ).astype(jnp.bfloat16)
    columns_all = lax.all_to_all(token_rows, CTX_DP, split_axis=1, concat_axis=0, tiled=True)
    summed = lax.dot_general(
        columns_all,
        lax.all_gather(grads_kv, CTX_DP, axis=0, tiled=True),
        (((0,), (0,)), ((), ())),
        preferred_element_type=jnp.float32,
    )
    key_weight_grad = summed[:, :head_size]
    value_weight_grad = summed[:, head_size:]
    attn_out = mixed.reshape(rows_here, head_count * head_size)[None]
    query_grad = query_acc.astype(jnp.bfloat16).reshape(rows_here, head_count * head_size)[None]
    return (attn_out, query_grad, token_grad[None], key_weight_grad, value_weight_grad)


def solution(mesh):
    torus = Mesh(mesh.devices.reshape(4, 2, 2, 4, 2), ("ctx_0", "ctx_1", "ctx_2", "dp_0", "dp_1"))
    in_specs = (
        P(DP, CTX, None),
        P(DP, CTX, None),
        P(DP, CTX, None),
        P(CTX_DP, None),
        P(CTX_DP, None),
        P(DP, None),
        P(DP, None),
    )
    out_specs = (
        P(DP, CTX, None),
        P(DP, CTX, None),
        P(DP, CTX, None),
        P(CTX_DP, None),
        P(CTX_DP, None),
    )
    return jax.shard_map(body, mesh=torus, in_specs=in_specs, out_specs=out_specs, check_vma=False)
```

profile of v0, /device:TPU:73, one launch (start us, length us, event | category | flops | bytes accessed | tf_op | source)
XLA Modules:
  0.0 1085.5 jit_solution(9353580749844137275)
XLA Ops:
  8.7 7.3 all-reduce.1
  16.0 5.9 all-reduce.4
  21.9 6.6 all-reduce.3
  28.5 9.1 all-reduce
  37.6 4.4 all-reduce.2
  45.8 314.5 %all-gather.4.cloned.1.call-done = bf16[16384,256]{1,0:T(8,128)(2,1)} async-done(((bf16[128,256]{1,0:T(8,128)(2,1)}), bf16[16384,256]{1,0:T(8,128)(2,1)}) %all-gather.4.cloned.1.call-update) | async-done | bytes 8388624 | tf_op jit(solution)/shard_map/all_gather | solution.py:94
  360.3 8.1 fusion.68
  371.4 44.9 %all-gather.6.cloned.1.call-done = bf16[2,4096,128]{1,2,0:T(8,128)(2,1)} async-done(((bf16[2,256,128]{1,2,0:T(8,128)(2,1)}), bf16[2,4096,128]{1,2,0:T(8,128)(2,1)}) %all-gather.6.cloned.1.call-update) | async-done | bytes 2097168 | tf_op jit(solution)/shard_map/all_gather | solution.py:22
  416.3 2.7 fusion.74
  424.7 62.8 %while.32 = (s32[]{:T(128)}, f32[8,256]{1,0:T(8,128)S(1)}, f32[8,256]{1,0:T(8,128)S(1)}, f32[256,8,128]{0,2,1:T(8,128)}, s32[8]{0:T(128)S(1)}, /*index=5*/s32[1,...) while((s32[]{:T(128)}, f32[8,256]{1,0:T(8,128)S(1)}, ...), condition=%wide.region_20.21_spmd.clone, body=%wide.region_15.20_spmd.clone.sunk | while | flops 551770112 | bytes 24531360 | solution.py:44
  429.2 2.4 fusion.121
  437.0 2.4 fusion.121
  444.9 2.4 fusion.121
  452.7 2.4 fusion.121
  460.6 2.4 fusion.121
  468.4 2.4 fusion.121
  489.7 80.0 %while.33 = (s32[]{:T(128)}, f32[256,8,128]{0,2,1:T(8,128)S(1)}, f32[8,512,256]{2,1,0:T(8,128)}, bf16[8,512,128]{2,1,0:T(8,128)(2,1)}, s32[8]{0:T(128)S(1)}, /*i...) while((s32[]{:T(128)}, f32[256,8,128]{0,2,1:T(8,128)S(1)}, ...), condition=%wide.region_25.26_spmd.clone, body=%wide.region_22.25_spmd.clone.sunk | while | flops 1354115072 | bytes 27570560 | solution.py:171
  569.8 77.3 %reduce-scatter.2.cloned.1.call-done = f32[256,256]{1,0:T(8,128)} async-done(((f32[4096,256]{1,0:T(8,128)}), f32[256,256]{1,0:T(8,128)}) %reduce-scatter.2.cloned.1.call-update) | async-done | bytes 262160 | tf_op jit(solution)/shard_map/reduce_scatter | solution.py:181
  648.7 11.9 %copy.87 = bf16[1,256,16384]{1,2,0:T(8,128)(2,1)} copy(bf16[1,256,16384]{2,1,0:T(8,128)(2,1)} %param.11) | data formatting | bytes 16777216 | tf_op args[0]
  660.6 114.3 %all_to_all.19 = bf16[256,128,128]{0,2,1:T(8,128)(2,1)} all-to-all(bf16[256,128,128]{0,2,1:T(8,128)(2,1)} %bitcast.195), channel_id=1, replica_groups=mesh['ctx_0'=4,'ctx_1'=2,'ctx_2'=2,'dp_0'=4,'dp_1'=2] {'ctx_0','ctx_1','..., dimensions={1} | all-to-all | bytes 16777216 | tf_op jit(solution)/shard_map/all_to_all | solution.py:187
  775.0 12.0 %copy.88 = bf16[128,256,128]{2,1,0:T(8,128)(2,1)} copy(bf16[128,256,128]{1,2,0:T(8,128)(2,1)} %bitcast.194) | data formatting | bytes 16777216 | tf_op jit(solution)/shard_map/all_to_all | solution.py:187
  789.0 9.2 fusion.62
  798.2 268.7 %all-gather.8.cloned.1.call-done = bf16[32768,256]{1,0:T(8,128)(2,1)} async-done(((bf16[256,256]{1,0:T(8,128)(2,1)}), bf16[32768,256]{1,0:T(8,128)(2,1)}) %all-gather.8.cloned.1.call-update) | async-done | bytes 16777232 | tf_op jit(solution)/shard_map/all_gather | solution.py:190
  1066.9 10.6 convolution_bitcast_fusion.1
  (292 shorter events, 136.9 us)
Async XLA Ops:
  7.2 353.1 %all-gather.4.cloned.1.call-start = ((), (), s32[]{:S(2)}) async-start(), calls=%async_computation.2 | async-start | bytes 8454144 | tf_op jit(solution)/shard_map/all_gather | solution.py:94
  45.7 323.8 %copy-start.8 = (s32[1,8]{1,0:T(1,128)S(1)}, s32[1,8]{1,0:T(1,128)}, u32[]{:S(2)}) copy-start(s32[1,8]{1,0:T(1,128)} %param.16) | copy-start | bytes 100
  45.7 323.9 %copy-start.5 = (bf16[1,256,1024]{2,1,0:T(8,128)(2,1)S(1)}, bf16[1,256,1024]{2,1,0:T(8,128)(2,1)}, u32[]{:S(2)}) copy-start(bf16[1,256,1024]{2,1,0:T(8,128)(2,1)} %param.12) | copy-start | bytes 1572868
  45.7 324.4 %copy-start.6 = (bf16[1,256,1024]{2,1,0:T(8,128)(2,1)S(1)}, bf16[1,256,1024]{2,1,0:T(8,128)(2,1)}, u32[]{:S(2)}) copy-start(bf16[1,256,1024]{2,1,0:T(8,128)(2,1)} %param.13) | copy-start | bytes 1572868
  45.7 325.4 %copy-start.7 = (s32[1,32]{1,0:T(1,128)S(1)}, s32[1,32]{1,0:T(1,128)}, u32[]{:S(2)}) copy-start(s32[1,32]{1,0:T(1,128)} %param.17) | copy-start | bytes 388
  45.7 370.6 %all-gather.6.cloned.1.call-start = ((), (), s32[]{:S(2)}) async-start(), calls=%async_computation.3 | async-start | bytes 2228224 | tf_op jit(solution)/shard_map/all_gather | solution.py:22
  369.2 277.9 %reduce-scatter.2.cloned.1.call-start = ((), (), s32[]{:S(2)}) async-start(), calls=%async_computation.4 | async-start | bytes 4456448 | tf_op jit(solution)/shard_map/reduce_scatter | solution.py:181
  424.7 62.8 %copy-start = (bf16[1,256,1024]{1,2,0:T(8,128)(2,1)S(1)}, bf16[1,256,1024]{1,2,0:T(8,128)(2,1)}, u32[]{:S(2)}) copy-start(bf16[1,256,1024]{1,2,0:T(8,128)(2,1)} %copy.82) | copy-start | bytes 1572868
  426.3 2.8 copy-start.3
  431.6 1.0 copy-start.4
  434.2 2.8 copy-start.3
  439.4 1.0 copy-start.4
  442.1 2.8 copy-start.3
  447.3 1.0 copy-start.4
  449.9 2.8 copy-start.3
  455.1 1.0 copy-start.4
  457.7 2.8 copy-start.3
  463.0 1.0 copy-start.4
  465.6 2.8 copy-start.3
  473.4 2.8 copy-start.3
  481.3 2.8 copy-start.3
  569.7 497.2 %all-gather.8.cloned.1.call-start = ((), (), s32[]{:S(2)}) async-start(), calls=%async_computation.5 | async-start | bytes 16908288 | tf_op jit(solution)/shard_map/all_gather | solution.py:190
  775.0 12.0 %copy-start.1 = (bf16[256,8,128]{0,2,1:T(8,128)(2,1)S(1)}, bf16[256,8,128]{0,2,1:T(8,128)(2,1)}, u32[]{:S(2)}) copy-start(bf16[256,8,128]{0,2,1:T(8,128)(2,1)} %get-tuple-element.642) | copy-start | bytes 1572868
  775.0 14.1 %copy-start.2 = (bf16[256,256]{1,0:T(8,128)(2,1)S(1)}, bf16[256,256]{1,0:T(8,128)(2,1)}, u32[]{:S(2)}) copy-start(bf16[256,256]{1,0:T(8,128)(2,1)} %convert_element_type.72) | copy-start | bytes 393220
  (3 other events, 2.9 us)
Sparse Core Ops, SparseCore 0:
  45.8 314.4 all-gather.3
  369.3 46.9 all-gather.5
  569.9 77.1 reduce-scatter.1
  648.8 418.0 all-gather.7
where the time goes:
time: 1090 us
  waiting for transfers between devices  705 us (65%)
  blocking collectives  148 us (14%)
  matrix products  119 us (11%)
  local copies, waits for them, and re-layouts  62.5 us (6%)
  other arithmetic  23.8 us (2%)
  between operations  15.3 us (1%)
  loops' own time  11.6 us (1%)
    all_gather x1, waiting for transfers between devices, body(): both = lax.all_gather(local_rows, CTX_DP, axis=0, tiled=True)  315 us
    all_gather x1, waiting for transfers between devices, body(): lax.all_gather(grads_kv, CTX_DP, axis=0, tiled=True)  269 us
    all_to_all x1, blocking collectives, body(): lax.all_to_all(token_rows, CTX_DP, split_axis=1, concat_axis=0, tiled=True)  114 us
    reduce_scatter x1, waiting for transfers between devices, body(): lax.psum_scatter(key_terms, CTX, scatter_dimension=0, tiled=True)  77.3 us
    all_gather x1, waiting for transfers between devices, in_one_piece(): result, at, done = (lax.all_gather(both, axis, axis=dim, tiled=True), 0, [])  44.9 us
    psum x5, blocking collectives, over_axes(): value = lax.psum(value, axis)  33.3 us
  transfers between devices with their start and end apart: 4, of which 4 were waited for; matrix products, arithmetic and copies ran while one was open for 3% of the time, Pallas kernels for 0%

commit v1 on v0

--- a/solution.py
+++ b/solution.py
@@ -91,7 +91,9 @@
         ],
         axis=1,
     )
-    both = lax.all_gather(local_rows, CTX_DP, axis=0, tiled=True)
+    both = jnp.concatenate(
+        lax.all_to_all(jnp.stack([local_rows] * lax.axis_size(CTX_DP)), CTX_DP, 0, 0), axis=0
+    )
     projected = jnp.dot(token_rows, both, preferred_element_type=jnp.float32).astype(jnp.bfloat16)
     key_pair = (projected[:, :head_size][None], projected[:, head_size:][None])
     query_heads = queries[0].reshape(rows_here, head_count, head_size)

time: 1090 us -> 879 us (0.81)
  waiting for transfers between devices: 705 us -> 390 us
  blocking collectives: 148 us -> 252 us
    all_gather x1 -> x0, waiting for transfers between devices: 315 us -> none  [body(): both = lax.all_gather(local_rows, CTX_DP, axis=0, tiled=True)]
    all_to_all x0 -> x1, blocking collectives: none -> 105 us  [body(): lax.all_to_all(jnp.stack([local_rows] * lax.axis_size(CTX_DP)), CTX_DP, 0...]
  transfers between devices with their start and end apart: 4 -> 3, of which waited for: 4 -> 3; matrix products, arithmetic and copies ran while one was open for 3% -> 4% of each run, Pallas kernels for 0% -> 0%
where the time goes in v1:
time: 879 us; the launch traced here: 876 us
  waiting for transfers between devices  390 us (44%)
  blocking collectives  252 us (29%)
  matrix products  120 us (14%)
  local copies, waits for them, and re-layouts  63.5 us (7%)
  other arithmetic  23.2 us (3%)
  between operations  15.2 us (2%)
  loops' own time  11.6 us (1%)
    all_gather x1, waiting for transfers between devices, body(): lax.all_gather(grads_kv, CTX_DP, axis=0, tiled=True)  267 us
    all_to_all x1, blocking collectives, body(): lax.all_to_all(token_rows, CTX_DP, split_axis=1, concat_axis=0, tiled=True)  114 us
    all_to_all x1, blocking collectives, body(): lax.all_to_all(jnp.stack([local_rows] * lax.axis_size(CTX_DP)), CTX_DP, 0...  105 us
    reduce_scatter x1, waiting for transfers between devices, body(): lax.psum_scatter(key_terms, CTX, scatter_dimension=0, tiled=True)  77.3 us
    all_gather x1, waiting for transfers between devices, in_one_piece(): result, at, done = (lax.all_gather(both, axis, axis=dim, tiled=True), 0, [])  45.8 us
    psum x5, blocking collectives, over_axes(): value = lax.psum(value, axis)  33.3 us
    unnamed x26, local copies, waits for them, and re-layouts  20.6 us
    dot_general x8, matrix products, forward_block(): jnp.einsum('hts,sd->thd', weights.astype(jnp.bfloat16), value_block, pref...  19 us
  transfers between devices with their start and end apart: 3, of which 3 were waited for; matrix products, arithmetic and copies ran while one was open for 4% of the time, Pallas kernels for 0%

profile of v1, /device:TPU:73, one launch (start us, length us, event | category | flops | bytes accessed | tf_op | source)
XLA Modules:
  0.0 876.3 jit_solution(229647358590829265)
XLA Ops:
  8.7 7.3 all-reduce.1
  16.0 5.9 all-reduce.4
  21.9 6.6 all-reduce.3
  28.5 9.1 %all-reduce = (f32[]{:T(128)}, f32[]{:T(128)}) all-reduce(f32[]{:T(128)} %get-tuple-element.635, f32[]{:T(128)} %get-tuple-element.636), channel_id=1, replica_groups=mesh['ctx_0'=4,'ctx_1'=2,'ctx_2'=2,'dp_0'=4,'dp_1'=2] {'dp_0'}, use_global_device_ids=true, to_apply=%region_10.11 | all-reduce | flops 2 | bytes 16 | tf_op jit(solution)/shard_map/psum | solution.py:16
  37.6 4.4 all-reduce.2
  46.1 105.0 %all_to_all.24 = bf16[128,128,256]{2,1,0:T(8,128)(2,1)S(1)} all-to-all(bf16[128,128,256]{2,1,0:T(8,128)(2,1)S(1)} %stack.2), channel_id=1, replica_groups=mesh['ctx_0'=4,'ctx_1'=2,'ctx_2'=2,'dp_0'=4,'dp_1'=2] {'ctx_0','ctx_1','..., dimensions={0} | all-to-all | bytes 16777216 | tf_op jit(solution)/shard_map/all_to_all | solution.py:95
  151.1 9.1 %fusion.68 = bf16[256,256]{0,1:T(8,128)(2,1)S(1)} fusion(bf16[16384,256]{1,0:T(8,128)(2,1)S(1)} %bitcast.195, bf16[1,256,16384]{2,1,0:T(8,128)(2,1)} %param.11), kind=kOutput, calls=%fused_computation.91 | convolution fusion | flops 2147549184 | bytes 16908288 | tf_op jit(solution)/shard_map/dot_general | solution.py:97
  163.1 45.8 %all-gather.3.cloned.1.call-done = bf16[2,4096,128]{1,2,0:T(8,128)(2,1)} async-done(((bf16[2,256,128]{1,2,0:T(8,128)(2,1)}), bf16[2,4096,128]{1,2,0:T(8,128)(2,1)}) %all-gather.3.cloned.1.call-update) | async-done | bytes 2097168 | tf_op jit(solution)/shard_map/all_gather | solution.py:22
  208.9 2.7 fusion.74
  217.3 62.8 %while.32 = (s32[]{:T(128)}, f32[8,256]{1,0:T(8,128)S(1)}, f32[8,256]{1,0:T(8,128)S(1)}, f32[256,8,128]{0,2,1:T(8,128)}, s32[8]{0:T(128)S(1)}, /*index=5*/s32[1,...) while((s32[]{:T(128)}, f32[8,256]{1,0:T(8,128)S(1)}, ...), condition=%wide.region_20.21_spmd.clone, body=%wide.region_15.20_spmd.clone.sunk | while | flops 551770112 | bytes 24531360 | solution.py:44
  221.8 2.4 fusion.121
  229.6 2.4 fusion.121
  237.5 2.4 fusion.121
  245.3 2.4 fusion.121
  253.1 2.4 fusion.121
  261.0 2.4 fusion.121
  282.3 80.0 %while.33 = (s32[]{:T(128)}, f32[256,8,128]{0,2,1:T(8,128)S(1)}, f32[8,512,256]{2,1,0:T(8,128)}, bf16[8,512,128]{2,1,0:T(8,128)(2,1)}, s32[8]{0:T(128)S(1)}, /*i...) while((s32[]{:T(128)}, f32[256,8,128]{0,2,1:T(8,128)S(1)}, ...), condition=%wide.region_25.26_spmd.clone, body=%wide.region_22.25_spmd.clone.sunk | while | flops 1354115072 | bytes 27570560 | solution.py:173
  362.4 77.3 %reduce-scatter.2.cloned.1.call-done = f32[256,256]{1,0:T(8,128)} async-done(((f32[4096,256]{1,0:T(8,128)}), f32[256,256]{1,0:T(8,128)}) %reduce-scatter.2.cloned.1.call-update) | async-done | bytes 262160 | tf_op jit(solution)/shard_map/reduce_scatter | solution.py:183
  441.2 11.9 %copy.87 = bf16[1,256,16384]{1,2,0:T(8,128)(2,1)} copy(bf16[1,256,16384]{2,1,0:T(8,128)(2,1)} %param.11) | data formatting | bytes 16777216 | tf_op args[0]
  453.2 114.2 %all_to_all.25 = bf16[256,128,128]{0,2,1:T(8,128)(2,1)} all-to-all(bf16[256,128,128]{0,2,1:T(8,128)(2,1)} %bitcast.198), channel_id=1, replica_groups=mesh['ctx_0'=4,'ctx_1'=2,'ctx_2'=2,'dp_0'=4,'dp_1'=2] {'ctx_0','ctx_1','..., dimensions={1} | all-to-all | bytes 16777216 | tf_op jit(solution)/shard_map/all_to_all | solution.py:189
  567.4 12.0 %copy.88 = bf16[128,256,128]{2,1,0:T(8,128)(2,1)} copy(bf16[128,256,128]{1,2,0:T(8,128)(2,1)} %bitcast.197) | data formatting | bytes 16777216 | tf_op jit(solution)/shard_map/all_to_all | solution.py:189
  581.4 9.2 %fusion.62 = bf16[1,256,16384]{2,1,0:T(8,128)(2,1)} fusion(bf16[256,256]{1,0:T(8,128)(2,1)S(1)} %copy-done.3, bf16[16384,256]{1,0:T(8,128)(2,1)} %bitcast.196), kind=kOutput, calls=%fused_computation.87 | convolution fusion | flops 2151677952 | bytes 16908288 | tf_op jit(solution)/shard_map/dot_general | solution.py:186
  590.6 267.1 %all-gather.5.cloned.1.call-done = bf16[32768,256]{1,0:T(8,128)(2,1)} async-done(((bf16[256,256]{1,0:T(8,128)(2,1)}), bf16[32768,256]{1,0:T(8,128)(2,1)}) %all-gather.5.cloned.1.call-update) | async-done | bytes 16777232 | tf_op jit(solution)/shard_map/all_gather | solution.py:192
  857.7 10.6 %convolution_bitcast_fusion.1 = f32[128,256]{0,1:T(8,128)S(1)} fusion(bf16[32768,256]{1,0:T(8,128)(2,1)} %all-gather.5.cloned.1.call-done, bf16[32768,128]{1,0:T(8,128)(2,1)} %bitcast.194), kind=kOutput, calls=%fused_computation.92 | convolution fusion | flops 2147483648 | bytes 25296896 | tf_op jit(solution)/shard_map/dot_general | solution.py:190
  (293 shorter events, 137.2 us)
Async XLA Ops:
  7.2 201.7 %all-gather.3.cloned.1.call-start = ((), (), s32[]{:S(2)}) async-start(), calls=%async_computation.3 | async-start | bytes 2228224 | tf_op jit(solution)/shard_map/all_gather | solution.py:22
  151.0 9.1 %copy-start = (bf16[128,128,256]{2,1,0:T(8,128)(2,1)}, bf16[128,128,256]{2,1,0:T(8,128)(2,1)S(1)}, u32[]{:S(2)}) copy-start(bf16[128,128,256]{2,1,0:T(8,128)(2,1)S(1)} %all_to_all.24) | copy-start | bytes 25165828
  151.1 10.1 %copy-start.9 = (s32[1,8]{1,0:T(1,128)S(1)}, s32[1,8]{1,0:T(1,128)}, u32[]{:S(2)}) copy-start(s32[1,8]{1,0:T(1,128)} %param.16) | copy-start | bytes 100
  151.1 10.3 %copy-start.6 = (bf16[1,256,1024]{2,1,0:T(8,128)(2,1)S(1)}, bf16[1,256,1024]{2,1,0:T(8,128)(2,1)}, u32[]{:S(2)}) copy-start(bf16[1,256,1024]{2,1,0:T(8,128)(2,1)} %param.12) | copy-start | bytes 1572868
  151.1 10.8 %copy-start.7 = (bf16[1,256,1024]{2,1,0:T(8,128)(2,1)S(1)}, bf16[1,256,1024]{2,1,0:T(8,128)(2,1)}, u32[]{:S(2)}) copy-start(bf16[1,256,1024]{2,1,0:T(8,128)(2,1)} %param.13) | copy-start | bytes 1572868
  151.1 11.8 %copy-start.8 = (s32[1,32]{1,0:T(1,128)S(1)}, s32[1,32]{1,0:T(1,128)}, u32[]{:S(2)}) copy-start(s32[1,32]{1,0:T(1,128)} %param.17) | copy-start | bytes 388
  160.9 278.8 %reduce-scatter.2.cloned.1.call-start = ((), (), s32[]{:S(2)}) async-start(), calls=%async_computation.4 | async-start | bytes 4456448 | tf_op jit(solution)/shard_map/reduce_scatter | solution.py:183
  217.3 62.8 %copy-start.1 = (bf16[1,256,1024]{1,2,0:T(8,128)(2,1)S(1)}, bf16[1,256,1024]{1,2,0:T(8,128)(2,1)}, u32[]{:S(2)}) copy-start(bf16[1,256,1024]{1,2,0:T(8,128)(2,1)} %copy.82) | copy-start | bytes 1572868
  218.9 2.8 copy-start.4
  224.1 1.0 copy-start.5
  226.8 2.8 copy-start.4
  232.0 1.0 copy-start.5
  234.6 2.8 copy-start.4
  239.8 1.0 copy-start.5
  242.5 2.8 copy-start.4
  247.7 1.0 copy-start.5
  250.3 2.8 copy-start.4
  255.5 1.0 copy-start.5
  258.2 2.8 copy-start.4
  266.0 2.8 copy-start.4
  273.9 2.8 copy-start.4
  362.3 495.4 %all-gather.5.cloned.1.call-start = ((), (), s32[]{:S(2)}) async-start(), calls=%async_computation.5 | async-start | bytes 16908288 | tf_op jit(solution)/shard_map/all_gather | solution.py:192
  567.4 12.0 %copy-start.2 = (bf16[256,8,128]{0,2,1:T(8,128)(2,1)S(1)}, bf16[256,8,128]{0,2,1:T(8,128)(2,1)}, u32[]{:S(2)}) copy-start(bf16[256,8,128]{0,2,1:T(8,128)(2,1)} %get-tuple-element.642) | copy-start | bytes 1572868
  567.4 14.1 %copy-start.3 = (bf16[256,256]{1,0:T(8,128)(2,1)S(1)}, bf16[256,256]{1,0:T(8,128)(2,1)}, u32[]{:S(2)}) copy-start(bf16[256,256]{1,0:T(8,128)(2,1)} %convert_element_type.72) | copy-start | bytes 393220
  (3 other events, 2.9 us)
Sparse Core Ops, SparseCore 0:
  161.0 47.8 all-gather.2
  362.4 77.1 reduce-scatter.1
  441.4 416.2 all-gather.4
